TPU v7x, 256 devices: a whole 4x4x8 slice. The times are simulated.
256 devices in a mesh: wide: 16 (over x_lo, y, core), narrow: 16 (over z, x_hi).
Axes of the slice: x: 4 (x_hi: 2, x_lo: 2; x = x_hi * 2 + x_lo), y: 4, z: 8, core: 2. Of those that a mesh axis runs over, the one named last changes fastest.
Arguments:
- coarse_basis: bfloat16 [32, 96, 3, 64, 8, 128], P('wide', None, None, 'narrow')
- material_ids: int32 [32, 64, 8, 128], P('wide', 'narrow'), may hold values from 0 to 15
- lame_table: bfloat16 [2, 16], replicated, may hold values from 0.5 to 4
- coarse_ids: int32 [32, 96], P('wide'), may hold values from 0 to 127, as said below
- coarse_slab: bfloat16 [98304, 2048], P('wide', 'narrow'), may hold values from -0.5 to 2.5, as said below
- panel_owner: int32 [1], replicated, may hold values from 0 to 14
Outputs:
- factored: bfloat16 [98304, 2048], P('wide', 'narrow')
- galerkin: float32 [32, 96, 96], P('wide')
Inputs may be any that keep to these rules, and one draw needn't show every extreme that they name: `coarse_ids`: the 96 numbers of a row are distinct. `coarse_slab`: for every column block t, the 128 x 128 block whose rows begin at t * 6144 is symmetric positive definite.
All inputs are finite; a program needn't handle non-finite values.
Results may differ from a plain program's by a relative error of at most 0.001.
The roundings to bfloat16 on the way count: a program that leaves them out, or rounds other values in their place, can miss the bound.
Values may be sent and summed in bfloat16 or wider, within the bound.
A program may use at most 192 MiB of HBM per device.

v0:
```python
import jax
import jax.numpy as jnp
from jax import lax
from jax.sharding import PartitionSpec as P


def padded_2(x, sides, width):
    for axis, dim in sides:
        count, length = (lax.axis_size(axis), x.shape[dim])
        up = [(i, (i + 1) % count) for i in range(count - 1)]
        down = [(j, i) for i, j in up]
        last = lax.slice_in_dim(x, length - width, length, axis=dim)
        initial = lax.slice_in_dim(x, 0, width, axis=dim)
        before = lax.ppermute(last, axis, up)
        after = lax.ppermute(initial, axis, down)
        x = jnp.concatenate([before, x, after], axis=dim)
    return x


def broadcast(value, axis, source):
    kept = jnp.where(lax.axis_index(axis) == source, value, 0).astype(value.dtype)
    return lax.psum(kept, axis)


def lower_inverse(lower):
    identity = jnp.eye(lower.shape[0], dtype=lower.dtype)
    return lax.linalg.triangular_solve(lower, identity, left_side=True, lower=True)


def lame_fields(material_ids, lame_table):
    values = lame_table.astype(jnp.float32)
    shear = jnp.zeros(material_ids.shape, jnp.float32)
    dilatation = jnp.zeros(material_ids.shape, jnp.float32)
    for material in range(values.shape[1]):
        chosen = material_ids == material
        shear = jnp.where(chosen, values[0, material], shear)
        dilatation = jnp.where(chosen, values[1, material], dilatation)
    return (shear, dilatation)


def shifted(field, axis, step):
    length = field.shape[axis]
    border = jnp.zeros_like(lax.slice_in_dim(field, 0, 1, axis=axis))
    if step > 0:
        return jnp.concatenate([lax.slice_in_dim(field, 1, length, axis=axis), border], axis=axis)
    return jnp.concatenate([border, lax.slice_in_dim(field, 0, length - 1, axis=axis)], axis=axis)


def face_weight(coeff_one, coeff_two, direction):
    shear = 0.5 * (coeff_one[:, 0:1] + coeff_two[:, 0:1])
    dilate = 0.5 * (coeff_one[:, 1:2] + coeff_two[:, 1:2])
    unit = (jnp.arange(3) == direction).astype(shear.dtype).reshape(1, 1, 3, 1, 1, 1)
    return shear + unit * (dilate + shear)


def operator_image(padded, coeff):
    centre = padded[:, :, :, 1:-1]
    coeff_centre = coeff[:, :, :, 1:-1]
    pairs = [
        (padded[:, :, :, 2:], coeff[:, :, :, 2:], 0),
        (padded[:, :, :, :-2], coeff[:, :, :, :-2], 0),
    ]
    for axis, direction in ((4, 1), (5, 2)):
        for step in (1, -1):
            pairs.append(
                (shifted(centre, axis, step), shifted(coeff_centre, axis, step), direction)
            )
    image = jnp.zeros(centre.shape, centre.dtype)
    for other, other_coeff, direction in pairs:
        image = image + face_weight(coeff_centre, other_coeff, direction) * (centre - other)
    return image


def galerkin_of(left_field, right_field):
    subs, funcs = (left_field.shape[0], left_field.shape[1])
    return jnp.einsum(
        "sak,sbk->sab",
        left_field.reshape(subs, funcs, -1),
        right_field.reshape(subs, funcs, -1),
        precision=lax.Precision.HIGHEST,
    )


def diagonal_factor(diagonal):
    diagonal = 0.5 * (diagonal + diagonal.T)
    lower = jnp.linalg.cholesky(diagonal)
    return (lower, lower_inverse(lower))


def panel_factor(column, lower, inverse, wide_index, owner, stride):
    solved = jnp.dot(column.astype(jnp.float32), inverse.T, precision=lax.Precision.HIGHEST)
    rows = lax.broadcasted_iota(jnp.int32, solved.shape, 0)
    head = rows < lower.shape[0]
    own_block = jnp.pad(lower, ((0, solved.shape[0] - lower.shape[0]), (0, 0)))
    diagonal_rows = head & (wide_index == owner * stride)
    earlier = head & (wide_index % stride == 0) & (wide_index // stride < owner)
    solved = jnp.where(diagonal_rows, own_block, solved)
    solved = jnp.where(earlier, 0.0, solved)
    return solved.astype(jnp.bfloat16)


def on_device(coarse_basis, material_ids, lame_table, coarse_ids, coarse_slab, panel_owner):
    narrow_count = lax.axis_size("narrow")
    stride = lax.axis_size("wide") // narrow_count
    wide_index = lax.axis_index("wide")
    narrow_index = lax.axis_index("narrow")
    owner = panel_owner[0]
    block = coarse_slab.shape[1]
    shear, dilatation = lame_fields(material_ids, lame_table)
    coeff = jnp.stack([shear, dilatation], 1)[:, :, None].astype(jnp.bfloat16)
    padded, coeff_padded = (
        padded_2(coarse_basis, (("narrow", 3),), 1),
        padded_2(coeff, (("narrow", 3),), 1),
    )
    padded = padded.astype(jnp.float32)
    image = operator_image(padded, coeff_padded.astype(jnp.float32))
    partial_sum = galerkin_of(padded[:, :, :, 1:-1], image)
    galerkin = lax.psum(partial_sum, "narrow")
    slots = (coarse_ids[:, :, None] == jnp.arange(block)[None, None, :]).astype(jnp.float32)
    spread = jnp.einsum("sab,sbc->sac", galerkin, slots, precision=lax.Precision.HIGHEST)
    added = jnp.einsum("sar,sac->rc", slots, spread, precision=lax.Precision.HIGHEST)
    assemble_here = (wide_index == narrow_index * stride) & (narrow_index >= owner)
    base = coarse_slab.astype(jnp.float32)
    base = base.at[:block].add(jnp.where(assemble_here, added, 0.0))
    diagonal = broadcast(base[:block], "wide", owner * stride)
    lower, inverse = diagonal_factor(diagonal)

    def owned():
        return panel_factor(coarse_slab, lower, inverse, wide_index, owner, stride)

    def empty_panel():
        return jnp.zeros(coarse_slab.shape, jnp.bfloat16)

    local_factor = lax.cond(narrow_index == owner, owned, empty_panel)
    factor = broadcast(local_factor, "narrow", owner)
    rows_needed = broadcast(factor[:block], "wide", narrow_index * stride)

    def updated():
        return base - jnp.einsum(
            "rk,ck->rc", factor, rows_needed, preferred_element_type=jnp.float32
        )

    def unchanged():
        return base

    result = lax.cond(narrow_index > owner, updated, unchanged)
    result = jnp.where(narrow_index == owner, factor.astype(jnp.float32), result)
    return (result.astype(jnp.bfloat16), galerkin)


def solution(mesh):
    return jax.shard_map(
        on_device,
        mesh=mesh,
        in_specs=(
            P("wide", None, None, "narrow", None, None),
            P("wide", "narrow", None, None),
            P(),
            P("wide", None),
            P("wide", "narrow"),
            P(),
        ),
        out_specs=(P("wide", "narrow"), P("wide", None, None)),
        check_vma=False,
    )
```

profile of v0, /device:TPU:32, one launch (start us, length us, event | category | flops | bytes accessed | tf_op | source)
XLA Modules:
  0.0 716.5 jit_solution(17513806060626854294)
XLA Ops:
  7.2 2.1 fusion.63
  9.3 1.8 fusion.64
  11.1 10.8 %select_convert_fusion.2 = (bf16[2,4,8,128]{3,2,1,0:T(8,128)(2,1)S(1)}, pred[2,4,8,128]{3,2,1,0:T(8,128)(4,1)S(1)}, pred[2,4,8,128]{3,2,1,0:T(8,128)(4,1)S(1)}, ...) fusion(bf16[]{:T(256)} %bitcast.16, ...), kind=kLoop, calls=%fused_computation.93 | loop fusion | flops 262144 | bytes 180256 | tf_op jit(solution)/shard_map/convert.7
  21.9 10.2 %select_convert_fusion.1 = bf16[2,4,8,128]{3,2,1,0:T(8,128)(2,1)S(1)} fusion(pred[2,4,8,128]{3,2,1,0:T(8,128)(4,1)S(1)} %get-tuple-element.65, pred[2,4,8,128]{3,2,1,0:T(8,128)(4,1)S(1)} %get-tuple-element.64, pred[2,4,8,128]{3,2,1,0:T(8,128)(4,1)S(1)} %get-tuple-element.63, pred[2,4,8,128]{3,2,1,0:T(8,128)(4,1)S(1)} %get-tuple-element.62, ...), kind=kLoop, calls=%fused_computation.92 | loop fusion | flops 131072 | bytes 147488 | tf_op jit(solution)/shard_map/convert.6
  32.7 4.9 collective-permute-start
  37.7 3.3 collective-permute-start.1
  41.0 2.1 fusion.60
  43.1 4.0 collective-permute-start.2
  47.1 4.2 collective-permute-start.3
  53.6 7.6 %reshape.222 = bf16[2,96,12288]{2,1,0:T(8,128)(2,1)} reshape(bf16[2,96,3,4,8,128]{5,4,3,2,1,0:T(8,128)(2,1)} %param.12) | data formatting | bytes 9437184 | tf_op jit(solution)/shard_map/reshape | solution.py:78
  63.7 33.3 %collective-permute-done.2 = bf16[2,96,3,1,8,128]{5,4,3,2,1,0:T(8,128)(2,1)S(1)} collective-permute-done((bf16[2,96,3,1,8,128]{5,4,3,2,1,0:T(8,128)(2,1)S(1)}, bf16[2,96,3,1,8,128]{5,4,3,2,1,0:T(8,128)(2,1)S(1)}, u32[]{:S(2)}, u32[]{:S(2)}) %collective-permute-start.2) | collective-permute-done | bytes 1179680 | tf_op jit(solution)/shard_map/ppermute | solution.py:14
  97.0 2.9 collective-permute-done.3
  99.9 9.3 %maximum_convert_fusion = f32[2,96,3,6,8,128]{5,4,3,2,1,0:T(8,128)} fusion(bf16[2,96,3,1,8,128]{5,4,3,2,1,0:T(8,128)(2,1)} %collective-permute-done.3, bf16[2,96,3,4,8,128]{5,4,3,2,1,0:T(8,128)(2,1)} %param.12, bf16[2,96,3,1,8,128]{5,4,3,2,1,0:T(8,128)(2,1)S(1)} %collective-permute-done.2), kind=kLoop, calls=%fused_computation.16 | loop fusion | flops 10616832 | bytes 21233664 | tf_op jit(solution)/shard_map/convert_element_type | solution.py:115
  109.2 14.4 %fusion.58 = (f32[2,96,3,4,7,128]{5,4,3,2,1,0:T(8,128)}, f32[2,96,3,4,7,128]{5,4,3,2,1,0:T(8,128)}) fusion(f32[2,96,3,6,8,128]{5,4,3,2,1,0:T(8,128)} %maximum_convert_fusion), kind=kLoop, calls=%fused_computation.123 | loop fusion | bytes 33030144 | tf_op jit(solution)/shard_map/slice | solution.py:45
  123.6 2.5 copy-done
  126.1 8.2 %fusion.59 = (f32[2,96,3,4,8,127]{5,4,3,2,1,0:T(8,128)}, f32[2,96,3,4,8,127]{5,4,3,2,1,0:T(8,128)}) fusion(f32[2,96,3,6,8,128]{5,4,3,2,1,0:T(8,128)S(1)} %copy-done), kind=kLoop, calls=%fused_computation.124 | loop fusion | bytes 37453824 | tf_op jit(solution)/shard_map/slice | solution.py:45
  134.3 27.3 %fusion.9 = f32[2,96,3,4,8,128]{5,4,3,2,1,0:T(8,128)} fusion(f32[2,96,3,6,8,128]{5,4,3,2,1,0:T(8,128)} %maximum_convert_fusion, f32[2,96,3,4,8,127]{5,4,3,2,1,0:T(8,128)} %get-tuple-element.71, f32[2,96,3,4,8,127]{5,4,3,2,1,0:T(8,128)} %get-tuple-element.70, f32[2,96,3,4,7,128]{5,4,3,2,1,0:T(8,128)} %get-tuple-element.69, ...), kind=kLoop, calls=%fused_computation.13 | loop fusion | flops 40108032 | bytes 73580544 | tf_op jit(solution)/shard_map/add | solution.py:70
  161.6 10.1 %reshape.221 = f32[2,96,12288]{2,1,0:T(8,128)} reshape(f32[2,96,3,4,8,128]{5,4,3,2,1,0:T(8,128)} %fusion.9) | data formatting | bytes 18874368 | tf_op jit(solution)/shard_map/reshape | solution.py:79
  171.7 10.1 %convolution_bitcast_fusion = f32[2,96,96]{1,2,0:T(8,128)} fusion(f32[2,96,12288]{2,1,0:T(8,128)} %reshape.221, bf16[2,96,12288]{2,1,0:T(8,128)(2,1)} %reshape.222), kind=kOutput, calls=%fused_computation.19 | convolution fusion | flops 2717908992 | bytes 14229504 | tf_op jit(solution)/shard_map/sak,sbk->sab/dot_general | solution.py:76
  182.5 1.6 convert_element_type.93
  184.1 159.0 %all-reduce.13.cloned.1.call-done = f32[2,96,96]{1,2,0:T(8,128)} async-done(((f32[2,96,96]{1,2,0:T(8,128)}), f32[2,96,96]{1,2,0:T(8,128)}) %all-reduce.13.cloned.1.call-update) | async-done | bytes 73744 | tf_op jit(solution)/shard_map/psum | solution.py:118
  343.1 1.2 fusion.13
  345.4 109.8 %all-reduce.15.cloned.1.call-done = f32[128,128]{1,0:T(8,128)} async-done(((f32[128,128]{1,0:T(8,128)}), f32[128,128]{1,0:T(8,128)}) %all-reduce.15.cloned.1.call-update) | async-done | bytes 65552 | tf_op jit(solution)/shard_map/psum | solution.py:22
  455.2 0.9 copy.8
  457.1 11.7 %cholesky.16 = f32[128,128]{1,0:T(8,128)S(1)} custom-call(f32[128,128]{1,0:T(8,128)S(1)} %fusion.16), custom_call_target="Cholesky" | custom-call | tf_op jit(solution)/shard_map/jit(cholesky)/cholesky | solution.py:86
  470.2 9.8 %custom-call.6 = f32[1,128,128]{1,2,0:T(8,128)S(1)} custom-call(f32[1,128,128]{2,1,0:T(8,128)S(1)} %get-tuple-element.47), custom_call_target="InvertDiagBlocksLowerTriangular" | custom-call | tf_op jit(solution)/shard_map/triangular_solve | solution.py:27
  480.2 1.4 conditional.2
  480.3 1.3 broadcast.208
  481.6 1.2 broadcast_select_fusion
  483.6 169.8 %all-reduce.17.cloned.1.call-done = bf16[6144,128]{1,0:T(8,128)(2,1)} async-done(((bf16[6144,128]{1,0:T(8,128)(2,1)}), bf16[6144,128]{1,0:T(8,128)(2,1)}) %all-reduce.17.cloned.1.call-update) | async-done | bytes 1572880 | tf_op jit(solution)/shard_map/psum | solution.py:22
  654.2 52.9 %psum.31 = bf16[128,128]{1,0:T(8,128)(2,1)S(1)} all-reduce(bf16[128,128]{1,0:T(8,128)(2,1)S(1)} %slice_select_fusion), channel_id=1, replica_groups=mesh['wide'=16,'narrow'=16] {'wide'}, use_global_device_ids=true, to_apply=%region_7.8 | all-reduce | flops 16384 | bytes 65536 | tf_op jit(solution)/shard_map/psum | solution.py:22
  707.1 2.9 select_convert_fusion
  (37 shorter events, 10.6 us)
Async XLA Ops:
  7.2 336.0 %all-reduce.13.cloned.1.call-start = ((), (), s32[]{:S(2)}) async-start(), calls=%async_computation | async-start | bytes 196608 | tf_op jit(solution)/shard_map/psum | solution.py:118
  32.7 28.5 %collective-permute-start = (bf16[2,2,1,1,8,128]{5,4,3,0,1,2:T(8,128)(2,1)}, bf16[2,2,1,1,8,128]{5,4,3,0,1,2:T(8,128)(2,1)S(1)}, u32[]{:S(2)}, u32[]{:S(2)}) collective-permute-start(bf16[2,2,1,1,8,128]{5,4,3,0,1,2:T(8,128)(2,1)} %get-tuple-element.96), channel_id=1, source_target_pairs={{0,1},{1,2},{2,3},{3,4},{4,5},{5,6},{6,7},{7,8},{8,9},{9,10},{10,1... | collective-permute-start | bytes 24584 | tf_op jit(solution)/shard_map/ppermute | solution.py:14
  37.7 23.5 %collective-permute-start.1 = (bf16[2,2,1,1,8,128]{5,4,3,0,1,2:T(8,128)(2,1)}, bf16[2,2,1,1,8,128]{5,4,3,0,1,2:T(8,128)(2,1)S(1)}, u32[]{:S(2)}, u32[]{:S(2)}) collective-permute-start(bf16[2,2,1,1,8,128]{5,4,3,0,1,2:T(8,128)(2,1)} %get-tuple-element.97), channel_id=1, source_target_pairs={{1,0},{2,1},{3,2},{4,3},{5,4},{6,5},{7,6},{8,7},{9,8},{10,9},{11,1... | collective-permute-start | bytes 24584 | tf_op jit(solution)/shard_map/ppermute | solution.py:15
  43.1 54.0 %collective-permute-start.2 = (bf16[2,96,3,1,8,128]{5,4,3,2,1,0:T(8,128)(2,1)S(1)}, bf16[2,96,3,1,8,128]{5,4,3,2,1,0:T(8,128)(2,1)S(1)}, u32[]{:S(2)}, u32[]{:S(2)}) collective-permute-start(bf16[2,96,3,1,8,128]{5,4,3,2,1,0:T(8,128)(2,1)S(1)} %get-tuple-element.72), channel_id=1, source_target_pairs={{0,1},{1,2},{2,3},{3,4},{4,5},{5,6},{6,7},{7,8},{8,9},{9,10},{10,1... | collective-permute-start | bytes 3538952 | tf_op jit(solution)/shard_map/ppermute | solution.py:14
  47.1 52.8 %collective-permute-start.3 = (bf16[2,96,3,1,8,128]{5,4,3,2,1,0:T(8,128)(2,1)S(1)}, bf16[2,96,3,1,8,128]{5,4,3,2,1,0:T(8,128)(2,1)}, u32[]{:S(2)}, u32[]{:S(2)}) collective-permute-start(bf16[2,96,3,1,8,128]{5,4,3,2,1,0:T(8,128)(2,1)S(1)} %get-tuple-element.73), channel_id=1, source_target_pairs={{1,0},{2,1},{3,2},{4,3},{5,4},{6,5},{7,6},{8,7},{9,8},{10,9},{11,1... | collective-permute-start | bytes 3538952 | tf_op jit(solution)/shard_map/ppermute | solution.py:15
  109.2 16.9 %copy-start = (f32[2,96,3,6,8,128]{5,4,3,2,1,0:T(8,128)S(1)}, f32[2,96,3,6,8,128]{5,4,3,2,1,0:T(8,128)}, u32[]{:S(2)}) copy-start(f32[2,96,3,6,8,128]{5,4,3,2,1,0:T(8,128)} %maximum_convert_fusion) | copy-start | bytes 42467332
  171.7 171.4 %copy-start.2 = (s32[2,96]{1,0:T(2,128)S(1)}, s32[2,96]{1,0:T(2,128)}, u32[]{:S(2)}) copy-start(s32[2,96]{1,0:T(2,128)} %param.15) | copy-start | bytes 2308
  181.8 273.4 %all-reduce.15.cloned.1.call-start = ((), (), s32[]{:S(2)}) async-start(), calls=%async_computation.1 | async-start | bytes 131072 | tf_op jit(solution)/shard_map/psum | solution.py:22
  345.4 308.0 %all-reduce.17.cloned.1.call-start = ((), (), s32[]{:S(2)}) async-start(), calls=%async_computation.2 | async-start | bytes 3145728 | tf_op jit(solution)/shard_map/psum | solution.py:22
  480.2 2.7 copy-start.1
Sparse Core Ops, SparseCore 0:
  181.9 161.1 all-reduce.12
  346.3 108.8 all-reduce.14
  483.0 170.3 all-reduce.16
where the time goes:
time: 718 us; the launch traced here: 716 us
  waiting for transfers between devices  475 us (66%)
  other arithmetic  93.7 us (13%)
  blocking collectives  52.9 us (7%)
  local copies, waits for them, and re-layouts  52 us (7%)
  starting transfers between devices  16.6 us (2%)
  between operations  14.6 us (2%)
  matrix products  11.9 us (2%)
    psum x2, waiting for transfers between devices, broadcast(): return lax.psum(kept, axis)  280 us
    psum x1, waiting for transfers between devices, on_device(): galerkin = lax.psum(partial_sum, 'narrow')  159 us
    psum x1, blocking collectives, broadcast(): return lax.psum(kept, axis)  52.9 us
    ppermute x2, waiting for transfers between devices, padded_2(): before = lax.ppermute(last, axis, up)  33.3 us
    add x1, other arithmetic, operator_image(): image + face_weight(coeff_centre, other_coeff, direction) * (centre - other)  27.3 us
    slice x4, local copies, waits for them, and re-layouts, shifted(): lax.slice_in_dim(field, 1, length, axis=axis)  22.7 us
    another operation x2, other arithmetic  21 us
  transfers between devices with their start and end apart: 7, of which 5 were waited for; matrix products, arithmetic and copies ran while one was open for 2% of the time, Pallas kernels for 0%

commit v1 on v0

--- a/solution.py
+++ b/solution.py
@@ -115,7 +115,7 @@
     padded = padded.astype(jnp.float32)
     image = operator_image(padded, coeff_padded.astype(jnp.float32))
     partial_sum = galerkin_of(padded[:, :, :, 1:-1], image)
-    galerkin = lax.psum(partial_sum, "narrow")
+    galerkin = jnp.sum(lax.all_gather(partial_sum, "narrow"), axis=0)
     slots = (coarse_ids[:, :, None] == jnp.arange(block)[None, None, :]).astype(jnp.float32)
     spread = jnp.einsum("sab,sbc->sac", galerkin, slots, precision=lax.Precision.HIGHEST)
     added = jnp.einsum("sar,sac->rc", slots, spread, precision=lax.Precision.HIGHEST)

time: 718 us -> 642 us (0.89)
  waiting for transfers between devices: 475 us -> 399 us
    psum x1 -> x0, waiting for transfers between devices: 159 us -> none  [on_device(): galerkin = lax.psum(partial_sum, 'narrow')]
    all_gather x0 -> x1, waiting for transfers between devices: none -> 82.4 us  [on_device(): galerkin = jnp.sum(lax.all_gather(partial_sum, 'narrow'), axis=0)]
  transfers between devices with their start and end apart: 7 -> 7, of which waited for: 5 -> 5; matrix products, arithmetic and copies ran while one was open for 2% -> 3% of each run, Pallas kernels for 0% -> 0%
where the time goes in v1:
time: 642 us; the launch traced here: 641 us
  waiting for transfers between devices  399 us (62%)
  other arithmetic  95.2 us (15%)
  blocking collectives  52.9 us (8%)
  local copies, waits for them, and re-layouts  52 us (8%)
  starting transfers between devices  16.6 us (3%)
  between operations  14.6 us (2%)
  matrix products  10.3 us (2%)
    psum x2, waiting for transfers between devices, broadcast(): return lax.psum(kept, axis)  280 us
    all_gather x1, waiting for transfers between devices, on_device(): galerkin = jnp.sum(lax.all_gather(partial_sum, 'narrow'), axis=0)  82.4 us
    psum x1, blocking collectives, broadcast(): return lax.psum(kept, axis)  52.9 us
    ppermute x2, waiting for transfers between devices, padded_2(): before = lax.ppermute(last, axis, up)  33.3 us
    add x1, other arithmetic, operator_image(): image + face_weight(coeff_centre, other_coeff, direction) * (centre - other)  27.3 us
    slice x4, local copies, waits for them, and re-layouts, shifted(): lax.slice_in_dim(field, 1, length, axis=axis)  22.7 us
    another operation x2, other arithmetic  21 us
  transfers between devices with their start and end apart: 7, of which 5 were waited for; matrix products, arithmetic and copies ran while one was open for 3% of the time, Pallas kernels for 0%

profile of v1, /device:TPU:32, one launch (start us, length us, event | category | flops | bytes accessed | tf_op | source)
XLA Modules:
  0.0 640.8 jit_solution(8836670541641481512)
XLA Ops:
  7.2 2.1 fusion.63
  9.3 1.8 fusion.64
  11.1 10.8 %select_convert_fusion.2 = (bf16[2,4,8,128]{3,2,1,0:T(8,128)(2,1)S(1)}, pred[2,4,8,128]{3,2,1,0:T(8,128)(4,1)S(1)}, pred[2,4,8,128]{3,2,1,0:T(8,128)(4,1)S(1)}, ...) fusion(bf16[]{:T(256)} %bitcast.16, ...), kind=kLoop, calls=%fused_computation.93 | loop fusion | flops 262144 | bytes 180256 | tf_op jit(solution)/shard_map/convert.7
  21.9 10.2 %select_convert_fusion.1 = bf16[2,4,8,128]{3,2,1,0:T(8,128)(2,1)S(1)} fusion(pred[2,4,8,128]{3,2,1,0:T(8,128)(4,1)S(1)} %get-tuple-element.65, pred[2,4,8,128]{3,2,1,0:T(8,128)(4,1)S(1)} %get-tuple-element.64, pred[2,4,8,128]{3,2,1,0:T(8,128)(4,1)S(1)} %get-tuple-element.63, pred[2,4,8,128]{3,2,1,0:T(8,128)(4,1)S(1)} %get-tuple-element.62, ...), kind=kLoop, calls=%fused_computation.92 | loop fusion | flops 131072 | bytes 147488 | tf_op jit(solution)/shard_map/convert.6
  32.7 4.9 collective-permute-start
  37.7 3.3 collective-permute-start.1
  41.0 2.1 fusion.60
  43.1 4.0 collective-permute-start.2
  47.1 4.2 collective-permute-start.3
  53.6 7.6 %reshape.222 = bf16[2,96,12288]{2,1,0:T(8,128)(2,1)} reshape(bf16[2,96,3,4,8,128]{5,4,3,2,1,0:T(8,128)(2,1)} %param.12) | data formatting | bytes 9437184 | tf_op jit(solution)/shard_map/reshape | solution.py:78
  63.7 33.3 %collective-permute-done.2 = bf16[2,96,3,1,8,128]{5,4,3,2,1,0:T(8,128)(2,1)S(1)} collective-permute-done((bf16[2,96,3,1,8,128]{5,4,3,2,1,0:T(8,128)(2,1)S(1)}, bf16[2,96,3,1,8,128]{5,4,3,2,1,0:T(8,128)(2,1)S(1)}, u32[]{:S(2)}, u32[]{:S(2)}) %collective-permute-start.2) | collective-permute-done | bytes 1179680 | tf_op jit(solution)/shard_map/ppermute | solution.py:14
  97.0 2.9 collective-permute-done.3
  99.9 9.3 %maximum_convert_fusion = f32[2,96,3,6,8,128]{5,4,3,2,1,0:T(8,128)} fusion(bf16[2,96,3,1,8,128]{5,4,3,2,1,0:T(8,128)(2,1)} %collective-permute-done.3, bf16[2,96,3,4,8,128]{5,4,3,2,1,0:T(8,128)(2,1)} %param.12, bf16[2,96,3,1,8,128]{5,4,3,2,1,0:T(8,128)(2,1)S(1)} %collective-permute-done.2), kind=kLoop, calls=%fused_computation.16 | loop fusion | flops 10616832 | bytes 21233664 | tf_op jit(solution)/shard_map/convert_element_type | solution.py:115
  109.2 14.4 %fusion.58 = (f32[2,96,3,4,7,128]{5,4,3,2,1,0:T(8,128)}, f32[2,96,3,4,7,128]{5,4,3,2,1,0:T(8,128)}) fusion(f32[2,96,3,6,8,128]{5,4,3,2,1,0:T(8,128)} %maximum_convert_fusion), kind=kLoop, calls=%fused_computation.123 | loop fusion | bytes 33030144 | tf_op jit(solution)/shard_map/slice | solution.py:45
  123.6 2.5 copy-done
  126.1 8.2 %fusion.59 = (f32[2,96,3,4,8,127]{5,4,3,2,1,0:T(8,128)}, f32[2,96,3,4,8,127]{5,4,3,2,1,0:T(8,128)}) fusion(f32[2,96,3,6,8,128]{5,4,3,2,1,0:T(8,128)S(1)} %copy-done), kind=kLoop, calls=%fused_computation.124 | loop fusion | bytes 37453824 | tf_op jit(solution)/shard_map/slice | solution.py:45
  134.3 27.3 %fusion.9 = f32[2,96,3,4,8,128]{5,4,3,2,1,0:T(8,128)} fusion(f32[2,96,3,6,8,128]{5,4,3,2,1,0:T(8,128)} %maximum_convert_fusion, f32[2,96,3,4,8,127]{5,4,3,2,1,0:T(8,128)} %get-tuple-element.71, f32[2,96,3,4,8,127]{5,4,3,2,1,0:T(8,128)} %get-tuple-element.70, f32[2,96,3,4,7,128]{5,4,3,2,1,0:T(8,128)} %get-tuple-element.69, ...), kind=kLoop, calls=%fused_computation.13 | loop fusion | flops 40108032 | bytes 73580544 | tf_op jit(solution)/shard_map/add | solution.py:70
  161.6 10.1 %reshape.221 = f32[2,96,12288]{2,1,0:T(8,128)} reshape(f32[2,96,3,4,8,128]{5,4,3,2,1,0:T(8,128)} %fusion.9) | data formatting | bytes 18874368 | tf_op jit(solution)/shard_map/reshape | solution.py:79
  171.7 9.4 %convolution_bitcast_fusion = f32[2,96,96]{1,2,0:T(8,128)S(1)} fusion(f32[2,96,12288]{2,1,0:T(8,128)} %reshape.221, bf16[2,96,12288]{2,1,0:T(8,128)(2,1)} %reshape.222), kind=kOutput, calls=%fused_computation.19 | convolution fusion | flops 2717908992 | bytes 14229504 | tf_op jit(solution)/shard_map/sak,sbk->sab/dot_general | solution.py:76
  182.6 1.6 convert_element_type.93
  184.2 82.4 %all-gather.3.cloned.1.call-done = f32[32,96,96]{2,1,0:T(8,128)} async-done(((f32[2,96,96]{2,1,0:T(8,128)}), f32[32,96,96]{2,1,0:T(8,128)}) %all-gather.3.cloned.1.call-update) | async-done | bytes 1179664 | tf_op jit(solution)/shard_map/all_gather | solution.py:118
  266.7 1.5 reduce_sum.9
  269.6 110.0 %all-reduce.12.cloned.1.call-done = f32[128,128]{1,0:T(8,128)} async-done(((f32[128,128]{1,0:T(8,128)}), f32[128,128]{1,0:T(8,128)}) %all-reduce.12.cloned.1.call-update) | async-done | bytes 65552 | tf_op jit(solution)/shard_map/psum | solution.py:22
  379.6 0.9 copy.12
  381.5 11.7 %cholesky.16 = f32[128,128]{1,0:T(8,128)S(1)} custom-call(f32[128,128]{1,0:T(8,128)S(1)} %fusion.16), custom_call_target="Cholesky" | custom-call | tf_op jit(solution)/shard_map/jit(cholesky)/cholesky | solution.py:86
  394.6 9.8 %custom-call.6 = f32[1,128,128]{1,2,0:T(8,128)S(1)} custom-call(f32[1,128,128]{2,1,0:T(8,128)S(1)} %get-tuple-element.47), custom_call_target="InvertDiagBlocksLowerTriangular" | custom-call | tf_op jit(solution)/shard_map/triangular_solve | solution.py:27
  404.7 1.4 conditional.2
  404.7 1.3 broadcast.208
  406.0 1.2 broadcast_select_fusion
  407.3 170.4 %all-reduce.14.cloned.1.call-done = bf16[6144,128]{1,0:T(8,128)(2,1)} async-done(((bf16[6144,128]{1,0:T(8,128)(2,1)}), bf16[6144,128]{1,0:T(8,128)(2,1)}) %all-reduce.14.cloned.1.call-update) | async-done | bytes 1572880 | tf_op jit(solution)/shard_map/psum | solution.py:22
  578.5 52.9 %psum.23 = bf16[128,128]{1,0:T(8,128)(2,1)S(1)} all-reduce(bf16[128,128]{1,0:T(8,128)(2,1)S(1)} %slice_select_fusion), channel_id=1, replica_groups=mesh['wide'=16,'narrow'=16] {'wide'}, use_global_device_ids=true, to_apply=%region_7.8 | all-reduce | flops 16384 | bytes 65536 | tf_op jit(solution)/shard_map/psum | solution.py:22
  631.4 2.9 select_convert_fusion
  (38 shorter events, 10.8 us)
Async XLA Ops:
  7.2 259.5 %all-gather.3.cloned.1.call-start = ((), (), s32[]{:S(2)}) async-start(), calls=%async_computation.2 | async-start | bytes 1671168 | tf_op jit(solution)/shard_map/all_gather | solution.py:118
  32.7 28.5 %collective-permute-start = (bf16[2,2,1,1,8,128]{5,4,3,0,1,2:T(8,128)(2,1)}, bf16[2,2,1,1,8,128]{5,4,3,0,1,2:T(8,128)(2,1)S(1)}, u32[]{:S(2)}, u32[]{:S(2)}) collective-permute-start(bf16[2,2,1,1,8,128]{5,4,3,0,1,2:T(8,128)(2,1)} %get-tuple-element.96), channel_id=1, source_target_pairs={{0,1},{1,2},{2,3},{3,4},{4,5},{5,6},{6,7},{7,8},{8,9},{9,10},{10,1... | collective-permute-start | bytes 24584 | tf_op jit(solution)/shard_map/ppermute | solution.py:14
  37.7 23.5 %collective-permute-start.1 = (bf16[2,2,1,1,8,128]{5,4,3,0,1,2:T(8,128)(2,1)}, bf16[2,2,1,1,8,128]{5,4,3,0,1,2:T(8,128)(2,1)S(1)}, u32[]{:S(2)}, u32[]{:S(2)}) collective-permute-start(bf16[2,2,1,1,8,128]{5,4,3,0,1,2:T(8,128)(2,1)} %get-tuple-element.97), channel_id=1, source_target_pairs={{1,0},{2,1},{3,2},{4,3},{5,4},{6,5},{7,6},{8,7},{9,8},{10,9},{11,1... | collective-permute-start | bytes 24584 | tf_op jit(solution)/shard_map/ppermute | solution.py:15
  43.1 54.0 %collective-permute-start.2 = (bf16[2,96,3,1,8,128]{5,4,3,2,1,0:T(8,128)(2,1)S(1)}, bf16[2,96,3,1,8,128]{5,4,3,2,1,0:T(8,128)(2,1)S(1)}, u32[]{:S(2)}, u32[]{:S(2)}) collective-permute-start(bf16[2,96,3,1,8,128]{5,4,3,2,1,0:T(8,128)(2,1)S(1)} %get-tuple-element.72), channel_id=1, source_target_pairs={{0,1},{1,2},{2,3},{3,4},{4,5},{5,6},{6,7},{7,8},{8,9},{9,10},{10,1... | collective-permute-start | bytes 3538952 | tf_op jit(solution)/shard_map/ppermute | solution.py:14
  47.1 52.8 %collective-permute-start.3 = (bf16[2,96,3,1,8,128]{5,4,3,2,1,0:T(8,128)(2,1)S(1)}, bf16[2,96,3,1,8,128]{5,4,3,2,1,0:T(8,128)(2,1)}, u32[]{:S(2)}, u32[]{:S(2)}) collective-permute-start(bf16[2,96,3,1,8,128]{5,4,3,2,1,0:T(8,128)(2,1)S(1)} %get-tuple-element.73), channel_id=1, source_target_pairs={{1,0},{2,1},{3,2},{4,3},{5,4},{6,5},{7,6},{8,7},{9,8},{10,9},{11,1... | collective-permute-start | bytes 3538952 | tf_op jit(solution)/shard_map/ppermute | solution.py:15
  109.2 16.9 %copy-start = (f32[2,96,3,6,8,128]{5,4,3,2,1,0:T(8,128)S(1)}, f32[2,96,3,6,8,128]{5,4,3,2,1,0:T(8,128)}, u32[]{:S(2)}) copy-start(f32[2,96,3,6,8,128]{5,4,3,2,1,0:T(8,128)} %maximum_convert_fusion) | copy-start | bytes 42467332
  171.7 96.5 %copy-start.2 = (s32[2,96]{1,0:T(2,128)S(1)}, s32[2,96]{1,0:T(2,128)}, u32[]{:S(2)}) copy-start(s32[2,96]{1,0:T(2,128)} %param.15) | copy-start | bytes 2308
  181.9 197.7 %all-reduce.12.cloned.1.call-start = ((), (), s32[]{:S(2)}) async-start(), calls=%async_computation | async-start | bytes 131072 | tf_op jit(solution)/shard_map/psum | solution.py:22
  268.2 139.1 %copy-start.1 = (f32[2,96,96]{2,1,0:T(8,128)}, f32[2,96,96]{2,1,0:T(8,128)S(1)}, u32[]{:S(2)}) copy-start(f32[2,96,96]{2,1,0:T(8,128)S(1)} %reduce_sum.9) | copy-start | bytes 221188
  269.5 308.2 %all-reduce.14.cloned.1.call-start = ((), (), s32[]{:S(2)}) async-start(), calls=%async_computation.1 | async-start | bytes 3145728 | tf_op jit(solution)/shard_map/psum | solution.py:22
Sparse Core Ops, SparseCore 0:
  182.0 84.6 all-gather.2
  269.9 109.7 all-reduce.11
  407.4 170.2 all-reduce.13
